TPU v7x, 32 devices: a whole 2x2x4 slice. The times are simulated.
32 devices in a mesh: row: 4 (over z), col: 8 (over y, x, core).
Axes of the slice: x: 2, y: 2, z: 4, core: 2. Of those that a mesh axis runs over, the one named last changes fastest.
Arguments:
- out_grads: bfloat16 [8, 48, 28672], P('col', None, 'row'), may hold values from -6 to 6
- acts: bfloat16 [8, 48, 8192], P('row', None, 'col'), may hold values from -6 to 6
- rot_out: bfloat16 [28672, 28672], P('row', 'col'), may hold values from -0.03125 to 0.03125
- rot_in: bfloat16 [8192, 8192], P('col', 'row'), may hold values from -0.0625 to 0.0625
- queries: bfloat16 [2, 28672, 8192], P(None, 'col', 'row'), may hold values from -0.00036621094 to 0.00036621094
- token_sequence: int32 [256], replicated, may hold values from 0 to 7, never falling along the last dimension, each value on 1 to 48 neighbouring positions
Outputs:
- scores: float32 [256, 2], P(('row', 'col'))
Inputs may be any that keep to these rules, and one draw needn't show every extreme that they name: `token_sequence`: values never fall along the tokens; every sequence 0 to 7 has 1 to 48 tokens, some sequence exactly 48; the k-th token of a sequence (from 0) sits in its slot k of out_grads and acts.
All inputs are finite; a program needn't handle non-finite values.
Results may differ from a plain program's by a relative error of at most 0.0041.
Values may be sent and summed in bfloat16 or wider, within the bound.
No kernel may reach another device: no remote copies, remote signals or barrier semaphores. Data moves between devices by JAX's collectives and lax.ppermute only.
A program may use at most 128 MiB of HBM per device.

v0:
```python
import jax
import jax.numpy as jnp
from jax import lax
from jax.sharding import PartitionSpec as P


def token_places(token_sequence, seq_count, slot_count):
    token_count = token_sequence.shape[0]
    labels = jnp.arange(seq_count, dtype=jnp.int32)
    before = (token_sequence[:, None] < labels[None, :]).astype(jnp.int32)
    starts = jnp.sum(before, axis=0)
    member = (token_sequence[:, None] == labels[None, :]).astype(jnp.int32)
    own_start = jnp.sum(member * starts[None, :], axis=1)
    position = jnp.arange(token_count, dtype=jnp.int32) - own_start
    return token_sequence * slot_count + position


def local(out_grads, acts, rot_out, rot_in, queries, token_sequence):
    slot_count = out_grads.shape[1]
    seq_count = out_grads.shape[0] * lax.axis_size("col")
    flat_index = token_places(token_sequence, seq_count, slot_count)
    act_slots = lax.all_gather(acts, "row", axis=0, tiled=True)
    act_rows = jnp.take(
        act_slots.reshape(seq_count * slot_count, act_slots.shape[2]), flat_index, axis=0
    )
    grad_slots = lax.all_gather(out_grads, "col", axis=0, tiled=True)
    grad_rows = jnp.take(
        grad_slots.reshape(seq_count * slot_count, grad_slots.shape[2]), flat_index, axis=0
    )
    picked = grad_rows
    rot_grads = lax.psum(
        jnp.dot(picked, rot_out, preferred_element_type=jnp.float32), "row"
    ).astype(jnp.bfloat16)
    picked = act_rows
    rot_acts = lax.psum(jnp.dot(picked, rot_in, preferred_element_type=jnp.float32), "col").astype(
        jnp.bfloat16
    )
    projected = jnp.einsum("tj,qij->tqi", rot_acts, queries, preferred_element_type=jnp.float32)
    score_terms = jnp.sum(projected * rot_grads[:, None, :], axis=2)
    return lax.psum_scatter(score_terms, ("row", "col"), scatter_dimension=0, tiled=True)


def solution(mesh):
    placed = (
        P("col", None, "row"),
        P("row", None, "col"),
        P("row", "col"),
        P("col", "row"),
        P(None, "col", "row"),
        P(),
    )
    return jax.shard_map(
        local, mesh=mesh, in_specs=placed, out_specs=P(("row", "col"), None), check_vma=False
    )
```

profile of v0, /device:TPU:0, one launch (start us, length us, event | category | flops | bytes accessed | tf_op | source)
XLA Modules:
  0.0 327.6 jit_solution(2703172752374178728)
XLA Ops:
  6.5 0.0 all-gather.2.cloned.1.call-start
  6.5 0.7 all-gather.2.cloned.1.call-update
  7.3 0.8 convert_reduce_fusion
  8.1 0.8 select_reduce_fusion
  8.8 0.7 compare_and_fusion
  9.5 21.5 %all_gather.6 = bf16[8,48,1024]{2,1,0:T(8,128)(2,1)S(1)} all-gather(bf16[2,48,1024]{2,1,0:T(8,128)(2,1)} %param.7), channel_id=1, replica_groups=mesh['row'=4,'col'=8] {'row'}, dimensions={0}, use_global_device_ids=true | all-gather | bytes 983040 | tf_op jit(solution)/shard_map/all_gather | solution.py:22
  31.0 1.2 gather_fusion
  32.2 3.5 %fusion.6 = f32[256,2048]{1,0:T(8,128)S(1)} fusion(bf16[1024,2048]{1,0:T(8,128)(2,1)} %param.9, bf16[256,1024]{1,0:T(8,128)(2,1)S(1)} %gather_fusion, pred[256]{0:T(512)(128)(4,1)S(1)} %get-tuple-element.5), kind=kOutput, calls=%fused_computation.10 | convolution fusion | flops 1074003968 | bytes 6816000 | tf_op jit(solution)/shard_map/dot_general | solution.py:35
  35.7 65.4 %all-reduce.4 = bf16[256,2048]{1,0:T(8,128)(2,1)S(1)} all-reduce(f32[256,2048]{1,0:T(8,128)S(1)} %fusion.6), channel_id=1, replica_groups=mesh['row'=4,'col'=8] {'col'}, use_global_device_ids=true, to_apply=%region_2.3 | all-reduce | flops 524288 | bytes 3145728 | tf_op jit(solution)/shard_map/psum | solution.py:35
  101.1 0.0 all-gather.2.cloned.1.call-done
  101.1 11.3 %gather_fusion.1 = bf16[256,7168]{1,0:T(8,128)(2,1)} fusion(bf16[384,7168]{1,0:T(8,128)(2,1)} %bitcast.10, s32[1024]{0:T(1024)S(1)} %pad_clamp_fusion), kind=kCustom, calls=%fused_computation.1 | custom fusion | bytes 7341056 | tf_op jit(solution)/shard_map/jit(_take)/gather | solution.py:27
  112.5 24.3 %fusion = f32[256,3584]{1,0:T(8,128)} fusion(bf16[7168,3584]{1,0:T(8,128)(2,1)} %param.8, bf16[256,7168]{1,0:T(8,128)(2,1)} %gather_fusion.1, pred[256]{0:T(512)(128)(4,1)S(1)} %get-tuple-element.5), kind=kOutput, calls=%fused_computation.3 | convolution fusion | flops 13155172352 | bytes 58720512 | tf_op jit(solution)/shard_map/dot_general | solution.py:32
  136.8 127.4 %all-reduce.3 = bf16[256,3584]{1,0:T(8,128)(2,1)S(1)} all-reduce(f32[256,3584]{1,0:T(8,128)} %fusion), channel_id=1, replica_groups=mesh['row'=4,'col'=8] {'row'}, use_global_device_ids=true, to_apply=%region_3.4 | all-reduce | flops 917504 | bytes 5505024 | tf_op jit(solution)/shard_map/psum | solution.py:31
  264.2 2.2 convert_element_type.25
  266.4 14.7 %multiply_reduce_fusion = f32[256,2]{0,1:T(2,128)S(1)} fusion(bf16[2,3584,2048]{2,1,0:T(8,128)(2,1)} %param.10, f32[256,3584]{1,0:T(8,128)} %convert_element_type.25, bf16[256,2048]{1,0:T(8,128)(2,1)S(1)} %all-reduce.4), kind=kOutput, calls=%fused_computation.2 | convolution fusion | flops 7519862272 | bytes 34080768 | tf_op jit(solution)/shard_map/tj,qij->tqi/dot_general | solution.py:38
  281.1 39.0 %all-reduce = f32[256,2]{0,1:T(2,128)S(1)} all-reduce(f32[256,2]{0,1:T(2,128)S(1)} %multiply_reduce_fusion), channel_id=2, replica_groups=mesh['row'=4,'col'=8] {'row','col'}, use_global_device_ids=true, to_apply=%region_5.6.clone | all-reduce | flops 512 | bytes 4096
  320.1 0.6 constant_dynamic-slice_fusion
  (1 shorter events, 0.0 us)
Async XLA Ops:
  6.5 94.6 %all-gather.2.cloned.1.call-start = ((), (), s32[]{:S(2)}) async-start(), calls=%async_computation | async-start | bytes 6193152 | tf_op jit(solution)/shard_map/all_gather | solution.py:26
Sparse Core Ops, SparseCore 0:
  9.2 56.0 all-gather.1
where the time goes:
time: 328 us
  blocking collectives  253 us (77%)
  matrix products  42.5 us (13%)
  between operations  13.5 us (4%)
  local copies, waits for them, and re-layouts  13.1 us (4%)
  other arithmetic  4.48 us (1%)
    psum x1, blocking collectives, local(): lax.psum(jnp.dot(picked, rot_out, preferred_element_type=jnp.float32), 'r...  127 us
    psum x1, blocking collectives, local(): lax.psum(jnp.dot(picked, rot_in, preferred_element_type=jnp.float32), 'col')  65.4 us
    unnamed x1, blocking collectives  39 us
    dot_general x1, matrix products, local(): jnp.dot(picked, rot_out, preferred_element_type=jnp.float32)  24.3 us
    all_gather x1, blocking collectives, local(): act_slots = lax.all_gather(acts, 'row', axis=0, tiled=True)  21.5 us
    dot_general x1, matrix products, local(): jnp.einsum('tj,qij->tqi', rot_acts, queries, preferred_element_type=jnp.f...  14.7 us
    gather x1, local copies, waits for them, and re-layouts, local(): jnp.take(grad_slots.reshape(seq_count * slot_count, grad_slots.shape[2]),...  11.3 us
  transfers between devices with their start and end apart: 1, of which 0 were waited for; matrix products, arithmetic and copies ran while one was open for 2% of the time, Pallas kernels for 0%

commit v1 on v0

--- a/solution.py
+++ b/solution.py
@@ -2,6 +2,10 @@
 import jax.numpy as jnp
 from jax import lax
 from jax.sharding import PartitionSpec as P
+
+
+def close_the_pools(payload):
+    return jnp.sum(lax.all_gather(payload, axis_name="col"), 0)
 
 
 def token_places(token_sequence, seq_count, slot_count):
@@ -32,7 +36,7 @@
         jnp.dot(picked, rot_out, preferred_element_type=jnp.float32), "row"
     ).astype(jnp.bfloat16)
     picked = act_rows
-    rot_acts = lax.psum(jnp.dot(picked, rot_in, preferred_element_type=jnp.float32), "col").astype(
+    rot_acts = close_the_pools(jnp.dot(picked, rot_in, preferred_element_type=jnp.float32)).astype(
         jnp.bfloat16
     )
     projected = jnp.einsum("tj,qij->tqi", rot_acts, queries, preferred_element_type=jnp.float32)

time: 328 us -> 292 us (0.89)
  blocking collectives: 253 us -> 190 us
  waiting for transfers between devices: 0.73 us -> 17.7 us
  other arithmetic: 4.48 us -> 12.2 us
    psum x1 -> x0, blocking collectives: 65.4 us -> none  [local(): lax.psum(jnp.dot(picked, rot_in, preferred_element_type=jnp.float32), 'col')]
    all_gather x1, waiting for transfers between devices: 0.02 us -> 17 us  [local(): grad_slots = lax.all_gather(out_grads, 'col', axis=0, tiled=True)]
    reduce_sum x0 -> x1, other arithmetic: none -> 7.77 us  [close_the_pools(): return jnp.sum(lax.all_gather(payload, axis_name='col'), 0)]
  transfers between devices with their start and end apart: 1 -> 2, of which waited for: 0 -> 1; matrix products, arithmetic and copies ran while one was open for 2% -> 16% of each run, Pallas kernels for 0% -> 0%
where the time goes in v1:
time: 292 us; the launch traced here: 291 us
  blocking collectives  190 us (65%)
  matrix products  44.5 us (15%)
  waiting for transfers between devices  17.7 us (6%)
  between operations  13.4 us (5%)
  local copies, waits for them, and re-layouts  13.1 us (4%)
  other arithmetic  12.2 us (4%)
    psum x1, blocking collectives, local(): lax.psum(jnp.dot(picked, rot_out, preferred_element_type=jnp.float32), 'r...  130 us
    unnamed x1, blocking collectives  38.2 us
    dot_general x1, matrix products, local(): jnp.dot(picked, rot_out, preferred_element_type=jnp.float32)  25 us
    all_gather x1, blocking collectives, local(): act_slots = lax.all_gather(acts, 'row', axis=0, tiled=True)  21.5 us
    all_gather x1, waiting for transfers between devices, local(): grad_slots = lax.all_gather(out_grads, 'col', axis=0, tiled=True)  17 us
    dot_general x1, matrix products, local(): jnp.einsum('tj,qij->tqi', rot_acts, queries, preferred_element_type=jnp.f...  14.7 us
    gather x1, local copies, waits for them, and re-layouts, local(): jnp.take(grad_slots.reshape(seq_count * slot_count, grad_slots.shape[2]),...  11.3 us
    reduce_sum x1, other arithmetic, close_the_pools(): return jnp.sum(lax.all_gather(payload, axis_name='col'), 0)  7.77 us
  transfers between devices with their start and end apart: 2, of which 1 were waited for; matrix products, arithmetic and copies ran while one was open for 16% of the time, Pallas kernels for 0%

profile of v1, /device:TPU:0, one launch (start us, length us, event | category | flops | bytes accessed | tf_op | source)
XLA Modules:
  0.0 291.2 jit_solution(1110403547237070251)
XLA Ops:
  6.5 0.0 all-gather.4.cloned.1.call-start
  6.5 0.7 all-gather.4.cloned.1.call-update
  7.3 0.0 all-gather.6.cloned.1.call-start
  7.3 0.8 convert_reduce_fusion
  8.1 0.8 select_reduce_fusion
  8.9 0.7 compare_and_fusion
  9.6 21.5 %all_gather.12 = bf16[8,48,1024]{2,1,0:T(8,128)(2,1)S(1)} all-gather(bf16[2,48,1024]{2,1,0:T(8,128)(2,1)} %param.7), channel_id=1, replica_groups=mesh['row'=4,'col'=8] {'row'}, dimensions={0}, use_global_device_ids=true | all-gather | bytes 983040 | tf_op jit(solution)/shard_map/all_gather | solution.py:26
  31.1 1.2 gather_fusion
  32.2 4.8 %fusion.6 = f32[256,2048]{1,0:T(8,128)} fusion(bf16[1024,2048]{1,0:T(8,128)(2,1)} %param.9, bf16[256,1024]{1,0:T(8,128)(2,1)S(1)} %gather_fusion, pred[256]{0:T(512)(128)(4,1)S(1)} %get-tuple-element.5), kind=kOutput, calls=%fused_computation.10 | convolution fusion | flops 1074003968 | bytes 6816000 | tf_op jit(solution)/shard_map/dot_general | solution.py:39
  37.0 0.0 all-gather.6.cloned.1.call-update
  37.1 17.0 %all-gather.4.cloned.1.call-done = bf16[8,48,7168]{2,1,0:T(8,128)(2,1)} async-done(((bf16[1,48,7168]{2,1,0:T(8,128)(2,1)}), bf16[8,48,7168]{2,1,0:T(8,128)(2,1)}) %all-gather.4.cloned.1.call-update) | async-done | bytes 5505040 | tf_op jit(solution)/shard_map/all_gather | solution.py:30
  54.1 11.3 %gather_fusion.1 = bf16[256,7168]{1,0:T(8,128)(2,1)} fusion(bf16[384,7168]{1,0:T(8,128)(2,1)} %bitcast.11, s32[1024]{0:T(1024)S(1)} %pad_clamp_fusion), kind=kCustom, calls=%fused_computation.1 | custom fusion | bytes 7341056 | tf_op jit(solution)/shard_map/jit(_take)/gather | solution.py:31
  65.4 25.0 %fusion = f32[256,3584]{1,0:T(8,128)} fusion(bf16[7168,3584]{1,0:T(8,128)(2,1)} %param.8, bf16[256,7168]{1,0:T(8,128)(2,1)} %gather_fusion.1, pred[256]{0:T(512)(128)(4,1)S(1)} %get-tuple-element.5), kind=kOutput, calls=%fused_computation.3 | convolution fusion | flops 13155172352 | bytes 58720512 | tf_op jit(solution)/shard_map/dot_general | solution.py:36
  90.4 130.4 %all-reduce.2 = bf16[256,3584]{1,0:T(8,128)(2,1)S(1)} all-reduce(f32[256,3584]{1,0:T(8,128)} %fusion), channel_id=1, replica_groups=mesh['row'=4,'col'=8] {'row'}, use_global_device_ids=true, to_apply=%region_3.4 | all-reduce | flops 917504 | bytes 5505024 | tf_op jit(solution)/shard_map/psum | solution.py:35
  220.8 2.2 convert_element_type.25
  223.0 0.0 all-gather.6.cloned.1.call-done
  223.0 7.8 %reduce_sum.38 = bf16[256,2048]{1,0:T(8,128)(2,1)S(1)} reduce(f32[8,256,2048]{2,1,0:T(8,128)} %bitcast.13, f32[]{:T(128)} %constant.33.clone.1), dimensions={0}, to_apply=%region_2.3 | reduce | flops 3670016 | bytes 17825796 | tf_op jit(solution)/shard_map/reduce_sum | solution.py:8
  230.8 14.7 %multiply_reduce_fusion = f32[256,2]{0,1:T(2,128)S(1)} fusion(bf16[2,3584,2048]{2,1,0:T(8,128)(2,1)} %param.10, f32[256,3584]{1,0:T(8,128)} %convert_element_type.25, bf16[256,2048]{1,0:T(8,128)(2,1)S(1)} %reduce_sum.38), kind=kOutput, calls=%fused_computation.2 | convolution fusion | flops 7519862272 | bytes 34080768 | tf_op jit(solution)/shard_map/tj,qij->tqi/dot_general | solution.py:42
  245.5 38.2 %all-reduce = f32[256,2]{0,1:T(2,128)S(1)} all-reduce(f32[256,2]{0,1:T(2,128)S(1)} %multiply_reduce_fusion), channel_id=3, replica_groups=mesh['row'=4,'col'=8] {'row','col'}, use_global_device_ids=true, to_apply=%region_5.6.clone | all-reduce | flops 512 | bytes 4096
  283.7 0.6 constant_dynamic-slice_fusion
  (1 shorter events, 0.0 us)
Async XLA Ops:
  6.5 47.5 %all-gather.4.cloned.1.call-start = ((), (), s32[]{:S(2)}) async-start(), calls=%async_computation | async-start | bytes 6193152 | tf_op jit(solution)/shard_map/all_gather | solution.py:30
  7.3 215.8 %all-gather.6.cloned.1.call-start = ((), (), s32[]{:S(2)}) async-start(), calls=%async_computation.1 | async-start | bytes 18874368 | tf_op jit(solution)/shard_map/all_gather | solution.py:8
Sparse Core Ops, SparseCore 0:
  9.2 44.7 all-gather.3
  55.9 89.7 all-gather.5
